TPU v7x, 256 devices: a whole 4x4x8 slice. The times are simulated.
256 devices in a mesh: outer: 8 (over x, y_lo), inner: 8 (over z), tensor: 4 (over y_hi, core).
Axes of the slice: x: 4, y: 4 (y_hi: 2, y_lo: 2; y = y_hi * 2 + y_lo), z: 8, core: 2. Of those that a mesh axis runs over, the one named last changes fastest.
Arguments:
- queries: bfloat16 [16384, 16, 128], P(('outer', 'inner'), 'tensor'), may hold values from -5 to 5
- keys: bfloat16 [16384, 4, 128], P(('outer', 'inner'), 'tensor'), may hold values from -5 to 5
- values: bfloat16 [16384, 4, 128], P(('outer', 'inner'), 'tensor'), may hold values from -6 to 6
- w_out: bfloat16 [16, 128, 4096], P('tensor'), may hold values from -0.125 to 0.125
- d_out: bfloat16 [16384, 4096], P(('outer', 'inner', 'tensor')), may hold values from -6 to 6
- lengths: int32 [16], replicated, may hold values from 1 to 10240, 16384 in all
Outputs:
- mixed: bfloat16 [16384, 4096], P(('outer', 'inner', 'tensor'))
- d_queries: bfloat16 [16384, 16, 128], P(('outer', 'inner'), 'tensor')
- d_keys: bfloat16 [16384, 4, 128], P(('outer', 'inner'), 'tensor')
- d_values: bfloat16 [16384, 4, 128], P(('outer', 'inner'), 'tensor')
Inputs may be any that keep to these rules, and one draw needn't show every extreme that they name: `lengths`: the 16 documents fill the sequence of 16384 tokens exactly, and the longest has exactly 10240 tokens.
All inputs are finite; a program needn't handle non-finite values.
Results may differ from a plain program's by a relative error of at most 0.04.
Values may be sent and summed in bfloat16 or wider, within the bound.
A program may use at most 128 MiB of HBM per device.

v0:
```python
import jax
import jax.numpy as jnp
from jax import lax
from jax.sharding import PartitionSpec as P

NEG_FILL = -1e30


def segment_of(positions, ends):
    return jnp.sum((positions[:, None] >= ends[None, :]).astype(jnp.int32), axis=1)


def doc_begin(position, ends):
    return jnp.max(jnp.where(ends <= position, ends, jnp.zeros_like(ends)))


def masked_scores(q_rows, k_block, q_pos, q_seg, k_start, ends, scale):
    width = k_block.shape[0]
    k_pos = k_start + jnp.arange(width, dtype=jnp.int32)
    k_seg = segment_of(k_pos, ends)
    s = (
        lax.dot_general(
            q_rows, k_block, (((1,), (1,)), ((), ())), preferred_element_type=jnp.float32
        )
        * scale
    )
    mask = (k_pos[None, :] <= q_pos[:, None]) & (k_seg[None, :] == q_seg[:, None])
    return (jnp.where(mask, s, NEG_FILL), mask)


def local(queries, keys, values, w_out, d_out, lengths):
    tok, heads_here, head_dim = queries.shape
    kv_here = keys.shape[1]
    group = heads_here // kv_here
    width = w_out.shape[2]
    ctx = lax.axis_size(("outer", "inner"))
    total = tok * ctx
    scale = head_dim ** (-0.5)
    offset = lax.axis_index(("outer", "inner")) * tok
    ends = jnp.cumsum(lengths)
    first = doc_begin(offset, ends)
    last = offset + tok - 1
    factor = 1
    while factor < ctx and tok * factor < 1024 and (ctx % (factor * 2) == 0):
        factor = factor * 2
    span = tok * factor
    n_blocks = total // span
    q_pos = offset + jnp.arange(tok * group, dtype=jnp.int32) // group
    q_seg = segment_of(q_pos, ends)
    key_all, value_all = (
        lax.all_gather(keys, ("outer", "inner"), axis=0, tiled=True),
        lax.all_gather(values, ("outer", "inner"), axis=0, tiled=True),
    )
    q_groups = queries.reshape(tok, kv_here, group, head_dim)
    zero = jnp.zeros((), jnp.int32)

    def needed(k_start, k_width):
        return (k_start <= last) & (k_start + k_width - 1 >= first)

    q_list = [q_groups[:, 0].reshape(tok * group, head_dim)]
    lse_list = []
    c = 0
    q_rows = q_list[c]

    def forward_block(b, carry, q_rows=q_rows, c=c):
        k_start = b * span

        def forward_work(state):
            top, denom, acc = state
            k_block = lax.dynamic_slice_in_dim(key_all, k_start, span, 0)[:, c]
            v_block = lax.dynamic_slice_in_dim(value_all, k_start, span, 0)[:, c]
            s, mask = masked_scores(q_rows, k_block, q_pos, q_seg, k_start, ends, scale)
            new_top = jnp.maximum(top, jnp.max(s, axis=1))
            weights = jnp.where(mask, jnp.exp(s - new_top[:, None]), 0.0)
            shrink = jnp.exp(top - new_top)
            denom = denom * shrink + jnp.sum(weights, axis=1)
            acc = acc * shrink[:, None] + jnp.dot(
                weights.astype(jnp.bfloat16), v_block, preferred_element_type=jnp.float32
            )
            return (new_top, denom, acc)

        return lax.cond(needed(k_start, span), forward_work, lambda st: st, carry)

    start_state = (
        jnp.full((tok * group,), NEG_FILL, jnp.float32),
        jnp.zeros((tok * group,), jnp.float32),
        jnp.zeros((tok * group, head_dim), jnp.float32),
    )
    top, denom, acc = lax.fori_loop(0, n_blocks, forward_block, start_state)
    attn_parts = [(acc / denom[:, None]).astype(jnp.bfloat16).reshape(tok, group, head_dim)]
    lse_list.append(top + jnp.log(denom))
    attn = jnp.stack(attn_parts, axis=1).reshape(tok, heads_here * head_dim)
    w_flat = w_out.reshape(heads_here * head_dim, width)
    mixed = lax.psum_scatter(
        jnp.dot(attn, w_flat, preferred_element_type=jnp.float32).astype(jnp.bfloat16),
        "tensor",
        scatter_dimension=0,
        tiled=True,
    )
    d_attn = lax.dot_general(
        lax.all_gather(d_out, "tensor", axis=0, tiled=True),
        w_flat,
        (((1,), (1,)), ((), ())),
        preferred_element_type=jnp.float32,
    ).astype(jnp.bfloat16)
    d_groups = d_attn.reshape(tok, kv_here, group, head_dim)
    a_groups = attn.reshape(tok, kv_here, group, head_dim)
    deltas = jnp.sum(d_groups.astype(jnp.float32) * a_groups.astype(jnp.float32), axis=3)
    g_list = [d_groups[:, 0].reshape(tok * group, head_dim)]
    delta_list = [deltas[:, 0].reshape(tok * group)]

    def grad_terms(c, k_start, k_width):
        k_block = lax.dynamic_slice_in_dim(key_all, k_start, k_width, 0)[:, c]
        v_block = lax.dynamic_slice_in_dim(value_all, k_start, k_width, 0)[:, c]
        s, mask = masked_scores(q_list[c], k_block, q_pos, q_seg, k_start, ends, scale)
        probs = jnp.where(mask, jnp.exp(s - lse_list[c][:, None]), 0.0)
        d_val = lax.dot_general(
            probs.astype(jnp.bfloat16),
            g_list[c],
            (((0,), (0,)), ((), ())),
            preferred_element_type=jnp.float32,
        )
        d_prob = lax.dot_general(
            g_list[c], v_block, (((1,), (1,)), ((), ())), preferred_element_type=jnp.float32
        )
        d_score = (probs * (d_prob - delta_list[c][:, None])).astype(jnp.bfloat16)
        dq_add = jnp.dot(d_score, k_block, preferred_element_type=jnp.float32) * scale
        d_key = (
            lax.dot_general(
                d_score, q_list[c], (((0,), (0,)), ((), ())), preferred_element_type=jnp.float32
            )
            * scale
        )
        return (dq_add, d_key, d_val)

    dq_start = tuple((jnp.zeros((tok * group, head_dim), jnp.float32) for c in range(kv_here)))

    def backward_block(b, carry):
        k_start = b * span

        def backward_work(state):
            dq_all, key_terms = state
            dq_add, d_key, d_val = grad_terms(0, k_start, span)
            new_dq = [dq_all[0] + dq_add]
            piece = jnp.stack((d_key, d_val), axis=1)[:, :, None, :]
            key_terms = lax.dynamic_update_slice(key_terms, piece, (k_start, zero, zero + 0, zero))
            return (tuple(new_dq), key_terms)

        return lax.cond(needed(k_start, span), backward_work, lambda st: st, carry)

    term_start = jnp.zeros((total, 2, kv_here, head_dim), jnp.float32)
    dq_all, key_terms = lax.fori_loop(0, n_blocks, backward_block, (dq_start, term_start))
    key_grads = lax.psum_scatter(key_terms, ("outer", "inner"), scatter_dimension=0, tiled=True)
    d_queries = (
        jnp.stack([d.reshape(tok, group, head_dim) for d in dq_all], axis=1)
        .reshape(tok, heads_here, head_dim)
        .astype(jnp.bfloat16)
    )
    d_keys = key_grads[:, 0].astype(jnp.bfloat16)
    d_values = key_grads[:, 1].astype(jnp.bfloat16)
    return (mixed, d_queries, d_keys, d_values)


def solution(mesh):
    return jax.shard_map(
        local,
        mesh=mesh,
        in_specs=(
            P(("outer", "inner"), "tensor", None),
            P(("outer", "inner"), "tensor", None),
            P(("outer", "inner"), "tensor", None),
            P("tensor", None, None),
            P(("outer", "inner", "tensor"), None),
            P(),
        ),
        out_specs=(
            P(("outer", "inner", "tensor"), None),
            P(("outer", "inner"), "tensor", None),
            P(("outer", "inner"), "tensor", None),
            P(("outer", "inner"), "tensor", None),
        ),
        check_vma=False,
    )
```

profile of v0, /device:TPU:1, one launch (start us, length us, event | category | flops | bytes accessed | tf_op | source)
XLA Modules:
  0.0 1233.0 jit_solution(10827884792633760065)
XLA Ops:
  9.4 0.7 copy.16
  11.1 32.1 %all-gather.8.cloned.1.call-done = bf16[256,4096]{1,0:T(8,128)(2,1)} async-done(((bf16[64,4096]{1,0:T(8,128)(2,1)}), bf16[256,4096]{1,0:T(8,128)(2,1)}) %all-gather.8.cloned.1.call-update) | async-done | bytes 2097168 | tf_op jit(solution)/shard_map/all_gather | solution.py:101
  43.2 4.1 convolution_convert_fusion.1
  47.7 253.0 %all-gather.4.cloned.1.call-done = bf16[16384,1,128]{2,0,1:T(8,128)(2,1)} async-done(((bf16[256,1,128]{2,0,1:T(8,128)(2,1)}), bf16[16384,1,128]{2,0,1:T(8,128)(2,1)}) %all-gather.4.cloned.1.call-update) | async-done | bytes 4194320 | tf_op jit(solution)/shard_map/all_gather | solution.py:51
  300.7 302.0 %all-gather.6.cloned.1.call-done = bf16[16384,1,128]{2,0,1:T(8,128)(2,1)} async-done(((bf16[256,1,128]{2,0,1:T(8,128)(2,1)}), bf16[16384,1,128]{2,0,1:T(8,128)(2,1)}) %all-gather.6.cloned.1.call-update) | async-done | bytes 4194320 | tf_op jit(solution)/shard_map/all_gather | solution.py:52
  602.7 17.8 %while.42 = (s32[]{:T(128)}, f32[1024]{0:T(1024)S(1)}, f32[1024]{0:T(1024)S(1)}, f32[1024,128]{1,0:T(8,128)S(1)}, s32[]{:T(128)}, /*index=5*/s32[]{:T(128)}, s32...) while((s32[]{:T(128)}, f32[1024]{0:T(1024)S(1)}, ...), condition=%wide.region_9.10_spmd.clone, body=%wide.region_3.9_spmd.clone.sunk | while | flops 560262144 | bytes 14574053 | solution.py:89
  603.3 6.7 conditional.6
  603.5 2.2 fusion.4
  605.7 1.6 fusion.6
  607.3 2.7 fusion.9
  621.2 6.0 broadcast_in_dim.31
  627.1 20.5 %while.43 = (s32[]{:T(128)}, f32[1024,128]{1,0:T(8,128)S(1)}, f32[16384,2,1,128]{3,0,1,2:T(8,128)}, s32[]{:T(128)}, s32[]{:T(128)}, /*index=5*/s32[16]{0:T(128)S...) while((s32[]{:T(128)}, f32[1024,128]{1,0:T(8,128)S(1)}, ...), condition=%wide.region_16.17_spmd.clone, body=%wide.region_12.16_spmd.clone.sunk | while | flops 1361765376 | bytes 24998396 | solution.py:152
  627.8 9.4 conditional.7
  628.0 1.7 fusion.39
  629.7 2.6 fusion.24
  632.3 1.3 fusion.31
  633.6 1.8 fusion.35
  635.4 0.7 fusion.34
  636.1 1.1 fusion.36
  647.9 4.8 convolution_convert_fusion
  652.7 0.7 convert_element_type.119
  653.4 483.7 %reduce-scatter.5.cloned.1.call-done = f32[256,2,1,128]{3,0,2,1:T(8,128)} async-done(((f32[16384,2,1,128]{3,0,2,1:T(8,128)}), f32[256,2,1,128]{3,0,2,1:T(8,128)}) %reduce-scatter.5.cloned.1.call-update) | async-done | bytes 262160 | tf_op jit(solution)/shard_map/reduce_scatter | solution.py:153
  1137.2 1.0 convert.6
  1138.8 87.6 %reduce-scatter.3.cloned.1.call-done = bf16[64,4096]{1,0:T(8,128)(2,1)} async-done(((bf16[256,4096]{1,0:T(8,128)(2,1)}), bf16[64,4096]{1,0:T(8,128)(2,1)}) %reduce-scatter.3.cloned.1.call-update) | async-done | bytes 524304 | tf_op jit(solution)/shard_map/reduce_scatter | solution.py:94
  (130 shorter events, 6.0 us)
Async XLA Ops:
  7.2 36.0 %all-gather.8.cloned.1.call-start = ((), (), s32[]{:S(2)}) async-start(), calls=%async_computation.5 | async-start | bytes 2621440 | tf_op jit(solution)/shard_map/all_gather | solution.py:101
  7.9 292.8 %all-gather.4.cloned.1.call-start = ((), (), s32[]{:S(2)}) async-start(), calls=%async_computation.2 | async-start | bytes 4259840 | tf_op jit(solution)/shard_map/all_gather | solution.py:51
  8.6 594.0 %all-gather.6.cloned.1.call-start = ((), (), s32[]{:S(2)}) async-start(), calls=%async_computation.3 | async-start | bytes 4259840 | tf_op jit(solution)/shard_map/all_gather | solution.py:52
  9.4 1127.8 %reduce-scatter.5.cloned.1.call-start = ((), (), s32[]{:S(2)}) async-start(), calls=%async_computation.6 | async-start | bytes 17039360 | tf_op jit(solution)/shard_map/reduce_scatter | solution.py:153
  43.2 559.5 %copy-start = (bf16[256,4,128]{2,1,0:T(4,128)(2,1)S(1)}, bf16[256,4,128]{2,1,0:T(4,128)(2,1)}, u32[]{:S(2)}) copy-start(bf16[256,4,128]{2,1,0:T(4,128)(2,1)} %param.14) | copy-start | bytes 786436
  647.7 578.8 %reduce-scatter.3.cloned.1.call-start = ((), (), s32[]{:S(2)}) async-start(), calls=%async_computation.4 | async-start | bytes 2621440 | tf_op jit(solution)/shard_map/reduce_scatter | solution.py:94
Sparse Core Ops, SparseCore 0:
  9.8 33.3 all-gather.7
  45.0 255.6 all-gather.3
  302.5 300.1 all-gather.5
  647.8 489.3 reduce-scatter.4
  1140.4 86.0 reduce-scatter.2
where the time goes:
time: 1230 us
  waiting for transfers between devices  1160 us (94%)
  loops' own time  22.2 us (2%)
  matrix products  21.9 us (2%)
  between operations  13.9 us (1%)
    reduce_scatter x1, waiting for transfers between devices, local(): lax.psum_scatter(key_terms, ('outer', 'inner'), scatter_dimension=0, tile...  484 us
    all_gather x1, waiting for transfers between devices, local(): lax.all_gather(values, ('outer', 'inner'), axis=0, tiled=True)  302 us
    all_gather x1, waiting for transfers between devices, local(): lax.all_gather(keys, ('outer', 'inner'), axis=0, tiled=True)  253 us
    reduce_scatter x1, waiting for transfers between devices, local(): lax.psum_scatter(jnp.dot(attn, w_flat, preferred_element_type=jnp.float32...  87.6 us
    all_gather x1, waiting for transfers between devices, local(): lax.all_gather(d_out, 'tensor', axis=0, tiled=True)  32.1 us
  transfers between devices with their start and end apart: 5, of which 5 were waited for; matrix products, arithmetic and copies ran while one was open for 1% of the time, Pallas kernels for 0%

commit v1 on v0

--- a/solution.py
+++ b/solution.py
@@ -49,7 +49,12 @@
     q_seg = segment_of(q_pos, ends)
     key_all, value_all = (
         lax.all_gather(keys, ("outer", "inner"), axis=0, tiled=True),
-        lax.all_gather(values, ("outer", "inner"), axis=0, tiled=True),
+        jnp.concatenate(
+            lax.all_to_all(
+                jnp.stack([values] * lax.axis_size(("outer", "inner"))), ("outer", "inner"), 0, 0
+            ),
+            axis=0,
+        ),
     )
     q_groups = queries.reshape(tok, kv_here, group, head_dim)
     zero = jnp.zeros((), jnp.int32)

time: 1230 us -> 960 us (0.78)
  waiting for transfers between devices: 1160 us -> 869 us
  starting transfers between devices: 0.19 us -> 14 us
    all_gather x1 -> x0, waiting for transfers between devices: 302 us -> none  [local(): lax.all_gather(values, ('outer', 'inner'), axis=0, tiled=True)]
    all_gather x1, waiting for transfers between devices: 253 us -> 269 us  [local(): lax.all_gather(keys, ('outer', 'inner'), axis=0, tiled=True)]
    all_to_all x0 -> x1, starting transfers between devices: none -> 13.9 us  [local(): lax.all_to_all(jnp.stack([values] * lax.axis_size(('outer', 'inner'))), (...]
  transfers between devices with their start and end apart: 5 -> 5, of which waited for: 5 -> 4; matrix products, arithmetic and copies ran while one was open for 1% -> 2% of each run, Pallas kernels for 0% -> 0%
where the time goes in v1:
time: 960 us; the launch traced here: 958 us
  waiting for transfers between devices  869 us (91%)
  loops' own time  22.2 us (2%)
  matrix products  22 us (2%)
  starting transfers between devices  14 us (1%)
  between operations  13.9 us (1%)
  local copies, waits for them, and re-layouts  11.3 us (1%)
    reduce_scatter x1, waiting for transfers between devices, local(): lax.psum_scatter(key_terms, ('outer', 'inner'), scatter_dimension=0, tile...  482 us
    all_gather x1, waiting for transfers between devices, local(): lax.all_gather(keys, ('outer', 'inner'), axis=0, tiled=True)  269 us
    reduce_scatter x1, waiting for transfers between devices, local(): lax.psum_scatter(jnp.dot(attn, w_flat, preferred_element_type=jnp.float32...  85.5 us
    all_gather x1, waiting for transfers between devices, local(): lax.all_gather(d_out, 'tensor', axis=0, tiled=True)  30.7 us
  transfers between devices with their start and end apart: 5, of which 4 were waited for; matrix products, arithmetic and copies ran while one was open for 2% of the time, Pallas kernels for 0%

profile of v1, /device:TPU:1, one launch (start us, length us, event | category | flops | bytes accessed | tf_op | source)
XLA Modules:
  0.0 958.2 jit_solution(13702867803250358716)
XLA Ops:
  8.6 3.8 stack.8
  12.4 13.9 %all-to-all-start = ((bf16[64,256,1,128]{3,1,2,0:T(8,128)(2,1)}), bf16[64,256,1,128]{3,1,2,0:T(8,128)(2,1)}, u32[]{:S(2)}, u32[]{:S(2)}) async-start(bf16[64,256,1,128]{3,1,2,0:T(8,128)(2,1)} %stack.8), calls=%async_computation | async-start | bytes 8388608 | tf_op jit(solution)/shard_map/all_to_all | solution.py:53
  27.4 30.7 %all-gather.5.cloned.1.call-done = bf16[256,4096]{1,0:T(8,128)(2,1)} async-done(((bf16[64,4096]{1,0:T(8,128)(2,1)}), bf16[256,4096]{1,0:T(8,128)(2,1)}) %all-gather.5.cloned.1.call-update) | async-done | bytes 2097168 | tf_op jit(solution)/shard_map/all_gather | solution.py:106
  58.0 4.1 convolution_convert_fusion.1
  62.5 268.7 %all-gather.3.cloned.1.call-done = bf16[16384,1,128]{2,0,1:T(8,128)(2,1)} async-done(((bf16[256,1,128]{2,0,1:T(8,128)(2,1)}), bf16[16384,1,128]{2,0,1:T(8,128)(2,1)}) %all-gather.3.cloned.1.call-update) | async-done | bytes 4194320 | tf_op jit(solution)/shard_map/all_gather | solution.py:51
  331.2 18.0 %while.42 = (s32[]{:T(128)}, f32[1024]{0:T(1024)S(1)}, f32[1024]{0:T(1024)S(1)}, f32[1024,128]{1,0:T(8,128)S(1)}, s32[]{:T(128)}, /*index=5*/s32[]{:T(128)}, s32...) while((s32[]{:T(128)}, f32[1024]{0:T(1024)S(1)}, ...), condition=%wide.region_9.10_spmd.clone, body=%wide.region_3.9_spmd.clone.sunk | while | flops 560262144 | bytes 14574053 | solution.py:94
  331.9 6.8 conditional.6
  332.1 2.3 fusion.4
  334.3 1.6 fusion.6
  336.0 2.8 fusion.9
  349.9 6.0 broadcast_in_dim.31
  355.9 20.5 %while.43 = (s32[]{:T(128)}, f32[1024,128]{1,0:T(8,128)S(1)}, f32[16384,2,1,128]{3,0,1,2:T(8,128)}, s32[]{:T(128)}, s32[]{:T(128)}, /*index=5*/s32[16]{0:T(128)S...) while((s32[]{:T(128)}, f32[1024,128]{1,0:T(8,128)S(1)}, ...), condition=%wide.region_16.17_spmd.clone, body=%wide.region_12.16_spmd.clone.sunk | while | flops 1361765376 | bytes 24998396 | solution.py:157
  356.5 9.4 conditional.7
  356.8 1.7 fusion.39
  358.4 2.6 fusion.24
  361.1 1.3 fusion.31
  362.4 1.8 fusion.35
  364.1 0.7 fusion.34
  364.9 1.1 fusion.36
  376.6 4.8 convolution_convert_fusion
  381.4 0.7 convert_element_type.119
  382.2 482.4 %reduce-scatter.5.cloned.1.call-done = f32[256,2,1,128]{3,0,2,1:T(8,128)} async-done(((f32[16384,2,1,128]{3,0,2,1:T(8,128)}), f32[256,2,1,128]{3,0,2,1:T(8,128)}) %reduce-scatter.5.cloned.1.call-update) | async-done | bytes 262160 | tf_op jit(solution)/shard_map/reduce_scatter | solution.py:158
  864.6 1.0 convert.6
  866.2 85.5 %reduce-scatter.3.cloned.1.call-done = bf16[64,4096]{1,0:T(8,128)(2,1)} async-done(((bf16[256,4096]{1,0:T(8,128)(2,1)}), bf16[64,4096]{1,0:T(8,128)(2,1)}) %reduce-scatter.3.cloned.1.call-update) | async-done | bytes 524304 | tf_op jit(solution)/shard_map/reduce_scatter | solution.py:99
  (132 shorter events, 5.4 us)
Async XLA Ops:
  7.2 50.9 %all-gather.5.cloned.1.call-start = ((), (), s32[]{:S(2)}) async-start(), calls=%async_computation.5 | async-start | bytes 2621440 | tf_op jit(solution)/shard_map/all_gather | solution.py:106
  7.9 323.3 %all-gather.3.cloned.1.call-start = ((), (), s32[]{:S(2)}) async-start(), calls=%async_computation.3 | async-start | bytes 4259840 | tf_op jit(solution)/shard_map/all_gather | solution.py:51
  12.4 13.9 %copy-start.1 = (s32[16]{0:T(128)S(1)}, s32[16]{0:T(128)}, u32[]{:S(2)}) copy-start(s32[16]{0:T(128)} %param.19) | copy-start | bytes 196
  12.4 318.8 %all-to-all-start = ((bf16[64,256,1,128]{3,1,2,0:T(8,128)(2,1)}), bf16[64,256,1,128]{3,1,2,0:T(8,128)(2,1)}, u32[]{:S(2)}, u32[]{:S(2)}) async-start(bf16[64,256,1,128]{3,1,2,0:T(8,128)(2,1)} %stack.8), calls=%async_computation | async-start | bytes 8388608 | tf_op jit(solution)/shard_map/all_to_all | solution.py:53
  26.3 838.2 %reduce-scatter.5.cloned.1.call-start = ((), (), s32[]{:S(2)}) async-start(), calls=%async_computation.6 | async-start | bytes 17039360 | tf_op jit(solution)/shard_map/reduce_scatter | solution.py:158
  58.0 273.2 %copy-start = (bf16[256,4,128]{2,1,0:T(4,128)(2,1)S(1)}, bf16[256,4,128]{2,1,0:T(4,128)(2,1)}, u32[]{:S(2)}) copy-start(bf16[256,4,128]{2,1,0:T(4,128)(2,1)} %param.14) | copy-start | bytes 786436
  376.4 575.3 %reduce-scatter.3.cloned.1.call-start = ((), (), s32[]{:S(2)}) async-start(), calls=%async_computation.4 | async-start | bytes 2621440 | tf_op jit(solution)/shard_map/reduce_scatter | solution.py:99
Sparse Core Ops, SparseCore 0:
  9.8 48.1 all-gather.4
  59.8 271.3 all-gather.2
  376.5 487.9 reduce-scatter.4
  867.8 83.8 reduce-scatter.2
